TPU v7x, 256 devices: a whole 4x4x8 slice. The times are simulated.
256 devices in a mesh: ctx: 64 (over x, y_lo, z), rep: 4 (over y_hi, core).
Axes of the slice: x: 4, y: 4 (y_hi: 2, y_lo: 2; y = y_hi * 2 + y_lo), z: 8, core: 2. Of those that a mesh axis runs over, the one named last changes fastest.
Arguments:
- tokens: bfloat16 [4, 8192, 2880], P('rep', 'ctx'), may hold values from -6 to 6
- router_w: bfloat16 [2880, 32], replicated, may hold values from -0.109375 to 0.109375
- router_b: float32 [32], replicated, may hold values from -4 to 4
- hidden: bfloat16 [4, 8192, 4, 1536], P('rep', 'ctx'), may hold values from -6 to 6
- teacher_idx: int32 [4, 8192, 4], P('rep', 'ctx'), may hold values from 0 to 31, all different within a row
- merge_map: int32 [32], replicated, may hold values from 0 to 15, as said below
- merge_coef: float32 [32], replicated, may hold values from 0.3 to 1.5
- source_w: bfloat16 [32, 1536, 1536], P(None, 'ctx'), may hold values from -0.15625 to 0.15625
- out_grad: bfloat16 [4, 8192, 1536], P('rep', 'ctx'), may hold values from -6 to 6
Outputs:
- mixed: bfloat16 [4, 8192, 1536], P('rep', 'ctx')
- hidden_grad: bfloat16 [4, 8192, 4, 1536], P('rep', 'ctx')
- token_grad: bfloat16 [4, 8192, 2880], P('rep', 'ctx')
- router_w_grad: float32 [2880, 32], replicated
- router_b_grad: float32 [32], replicated
- coef_grad: float32 [32], replicated
- source_w_grad: float32 [32, 1536, 1536], P(None, 'ctx', 'rep')
Inputs may be any that keep to these rules, and one draw needn't show every extreme that they name: `teacher_idx`: each token names 4 different experts. `merge_map`: each of the 16 combinations takes exactly two of the 32 experts.
All inputs are finite; a program needn't handle non-finite values.
Results may differ from a plain program's by a relative error of at most 0.0064.
Values may be sent and summed in bfloat16 or wider, within the bound.
A program may use at most 128 MiB of HBM per device.

v0:
```python
import math
import jax
import jax.numpy as jnp
from jax import lax
from jax.sharding import PartitionSpec as P

MERGED = 16


def expert_rows(rows_hidden, rows_grad, rows_member, lane_weights):
    row_count = rows_hidden.shape[0]
    out_rows = jnp.zeros((row_count, lane_weights.shape[1]), jnp.float32)
    back_rows = jnp.zeros((row_count, lane_weights.shape[2]), jnp.float32)
    weight = lane_weights[0]
    selected = (rows_member == 0)[:, None]
    forward = lax.dot_general(
        rows_hidden, weight, (((1,), (1,)), ((), ())), preferred_element_type=jnp.float32
    )
    out_rows = jnp.where(selected, forward, out_rows)
    backward = jnp.dot(rows_grad, weight, preferred_element_type=jnp.float32)
    back_rows = jnp.where(selected, backward, back_rows)
    masked = jnp.where(selected, rows_grad, jnp.zeros_like(rows_grad))
    grad_list = [
        lax.dot_general(
            masked, rows_hidden, (((0,), (0,)), ((), ())), preferred_element_type=jnp.float32
        )
    ]
    return (out_rows, back_rows, jnp.stack(grad_list))


def on_device(
    tokens, router_w, router_b, hidden, teacher_idx, merge_map, merge_coef, source_w, out_grad
):
    ctx_count = lax.axis_size("ctx")
    rep_count = lax.axis_size("rep")
    tok_count = tokens.shape[1]
    feature_count = tokens.shape[2]
    top_count = teacher_idx.shape[2]
    hidden_width = hidden.shape[3]
    out_width = out_grad.shape[2]
    source_count = router_w.shape[1]
    row_share = source_w.shape[1]
    per_lane = max(1, MERGED // ctx_count)
    copies = max(1, ctx_count // MERGED)
    capacity = 5 * tok_count * top_count // (4 * ctx_count)
    slot_count = tok_count * top_count
    grad_scale = 1.0 / math.sqrt(tok_count * ctx_count * rep_count)
    flat_x = tokens.reshape(tok_count, feature_count)
    logits = jnp.dot(flat_x, router_w, preferred_element_type=jnp.float32) + router_b
    choice_ids = teacher_idx.reshape(tok_count, top_count)
    pick_table = choice_ids[:, :, None] == jnp.arange(source_count, dtype=jnp.int32)[None, None, :]
    pick_float = pick_table.astype(jnp.float32)
    chosen = jnp.sum(pick_float * logits[:, None, :], axis=2)
    raised = jnp.exp(chosen)
    gate_probs = raised / jnp.sum(raised, axis=1, keepdims=True)
    merged_id = jnp.sum(jnp.where(pick_table, merge_map[None, None, :], 0), axis=2)
    position = lax.axis_index("ctx") * tok_count + jnp.arange(tok_count, dtype=jnp.int32)
    lane_id = merged_id // per_lane * copies + (position % copies)[:, None]
    member_id = (merged_id % per_lane).reshape(-1)
    lane_flat = lane_id.reshape(-1)
    onehot = (lane_flat[:, None] == jnp.arange(ctx_count, dtype=jnp.int32)[None, :]).astype(
        jnp.int32
    )
    before = jnp.cumsum(onehot, axis=0) - onehot
    slot_rank = jnp.sum(before * onehot, axis=1)
    is_kept = slot_rank < capacity
    slot_index = jnp.where(is_kept, lane_flat * capacity + slot_rank, ctx_count * capacity)
    slot_source = (
        jnp.full((ctx_count * capacity + 1,), slot_count, jnp.int32)
        .at[slot_index]
        .set(jnp.arange(slot_count, dtype=jnp.int32))[: ctx_count * capacity]
    )
    slot_grad = (gate_probs[:, :, None] * out_grad.reshape(tok_count, 1, out_width)).astype(
        jnp.bfloat16
    )
    pad_hidden = jnp.concatenate(
        [hidden.reshape(slot_count, hidden_width), jnp.zeros((1, hidden_width), jnp.bfloat16)],
        axis=0,
    )
    pad_grad = jnp.concatenate(
        [slot_grad.reshape(slot_count, out_width), jnp.zeros((1, out_width), jnp.bfloat16)], axis=0
    )
    pad_member = jnp.concatenate([member_id, jnp.zeros((1,), jnp.int32)], axis=0)
    send_hidden = pad_hidden[slot_source].reshape(ctx_count, capacity, hidden_width)
    send_grad = pad_grad[slot_source].reshape(ctx_count, capacity, out_width)
    send_member = pad_member[slot_source].reshape(ctx_count, capacity)
    lane_group = lax.axis_index("ctx") // copies
    same_group = merge_map[:, None] == merge_map[None, :]
    earlier = jnp.arange(source_count)[:, None] > jnp.arange(source_count)[None, :]
    member_rank = jnp.sum((same_group & earlier).astype(jnp.int32), axis=1)
    source_order = (
        jnp.zeros((source_count,), jnp.int32)
        .at[2 * merge_map + member_rank]
        .set(jnp.arange(source_count, dtype=jnp.int32))
    )
    picked = source_w[source_order].reshape(
        MERGED // per_lane, 2 * per_lane, row_share, hidden_width
    )
    outgoing = jnp.repeat(picked, copies, axis=0)
    arrived = lax.all_to_all(outgoing, "ctx", split_axis=0, concat_axis=2, tiled=True)
    coef_table = merge_coef[source_order].reshape(MERGED // per_lane, per_lane, 2)
    pair_coef = lax.dynamic_index_in_dim(coef_table, lane_group, 0, keepdims=False)
    lane_weights = (
        pair_coef[:, 0, None, None] * arrived[:, 0].astype(jnp.float32)
        + pair_coef[:, 1, None, None] * arrived[:, 1].astype(jnp.float32)
    ).astype(jnp.bfloat16)
    recv_hidden, recv_grad, recv_member = (
        lax.all_to_all(send_hidden, "ctx", split_axis=0, concat_axis=0, tiled=True),
        lax.all_to_all(send_grad, "ctx", split_axis=0, concat_axis=0, tiled=True),
        lax.all_to_all(send_member, "ctx", split_axis=0, concat_axis=0, tiled=True),
    )
    out_rows, back_rows, lane_grads = expert_rows(
        recv_hidden.reshape(-1, hidden_width),
        recv_grad.reshape(-1, out_width),
        recv_member.reshape(-1),
        lane_weights,
    )
    home_out, home_back = (
        lax.all_to_all(
            out_rows.astype(jnp.bfloat16).reshape(ctx_count, capacity, out_width),
            "ctx",
            split_axis=0,
            concat_axis=0,
            tiled=True,
        ),
        lax.all_to_all(
            back_rows.astype(jnp.bfloat16).reshape(ctx_count, capacity, hidden_width),
            "ctx",
            split_axis=0,
            concat_axis=0,
            tiled=True,
        ),
    )
    slot_out = jnp.concatenate(
        [home_out.reshape(-1, out_width), jnp.zeros((1, out_width), jnp.bfloat16)], axis=0
    )[slot_index].reshape(tok_count, top_count, out_width)
    hidden_grad = jnp.concatenate(
        [home_back.reshape(-1, hidden_width), jnp.zeros((1, hidden_width), jnp.bfloat16)], axis=0
    )[slot_index].reshape(1, tok_count, top_count, hidden_width)
    mixed = (
        jnp.sum(gate_probs[:, :, None] * slot_out.astype(jnp.float32), axis=1)
        .astype(jnp.bfloat16)
        .reshape(1, tok_count, out_width)
    )
    score_grad = jnp.einsum(
        "td,tkd->tk",
        out_grad.reshape(tok_count, out_width),
        slot_out,
        preferred_element_type=jnp.float32,
    )
    chosen_grad = gate_probs * (
        score_grad - jnp.sum(gate_probs * score_grad, axis=1, keepdims=True)
    )
    logit_grad = jnp.sum(pick_float * chosen_grad[:, :, None], axis=1)
    logit_half = logit_grad.astype(jnp.bfloat16)
    token_grad = (
        lax.dot_general(
            logit_half, router_w, (((1,), (1,)), ((), ())), preferred_element_type=jnp.float32
        )
        .astype(jnp.bfloat16)
        .reshape(1, tok_count, feature_count)
    )
    part_router_w = lax.dot_general(
        flat_x, logit_half, (((0,), (0,)), ((), ())), preferred_element_type=jnp.float32
    )
    part_router_b = jnp.sum(logit_grad, axis=0)
    arrived_grads = lax.all_to_all(
        lane_grads.reshape(per_lane, ctx_count, row_share, hidden_width),
        "ctx",
        split_axis=1,
        concat_axis=0,
        tiled=True,
    )
    merged_grad = (
        arrived_grads.reshape(MERGED // per_lane, copies, per_lane, row_share, hidden_width)
        .sum(axis=1)
        .reshape(MERGED, row_share, hidden_width)
    )
    source_grad = merged_grad[merge_map]
    coef_part = jnp.einsum(
        "edf,edf->e", source_grad, source_w.astype(jnp.float32), precision=lax.Precision.HIGHEST
    )
    summed = lax.psum_scatter(
        source_grad * merge_coef[:, None, None], "rep", scatter_dimension=2, tiled=True
    )
    source_w_grad = summed * grad_scale
    router_sum, bias_sum, coef_sum = lax.psum(
        (part_router_w, part_router_b, coef_part), ("ctx", "rep")
    )
    return (
        mixed,
        hidden_grad,
        token_grad,
        router_sum * grad_scale,
        bias_sum * grad_scale,
        coef_sum * grad_scale,
        source_w_grad,
    )


def solution(mesh):
    in_specs = (
        P("rep", "ctx", None),
        P(),
        P(),
        P("rep", "ctx", None, None),
        P("rep", "ctx", None),
        P(),
        P(),
        P(None, "ctx", None),
        P("rep", "ctx", None),
    )
    out_specs = (
        P("rep", "ctx", None),
        P("rep", "ctx", None, None),
        P("rep", "ctx", None),
        P(),
        P(),
        P(),
        P(None, "ctx", "rep"),
    )
    return jax.shard_map(
        on_device, mesh=mesh, in_specs=in_specs, out_specs=out_specs, check_vma=False
    )
```

profile of v0, /device:TPU:1, one launch (start us, length us, event | category | flops | bytes accessed | tf_op | source)
XLA Modules:
  0.0 1014.5 jit_solution(12828136133311541424)
XLA Ops:
  17.5 13.5 %all-to-all-start = ((s32[64,1,10]{2,1,0:T(1,128)}), s32[64,1,10]{2,1,0:T(1,128)S(1)}, u32[]{:S(2)}, u32[]{:S(2)}) async-start(s32[64,1,10]{2,1,0:T(1,128)} %bitcast.5), calls=%async_computation | async-start | bytes 65536 | tf_op jit(solution)/shard_map/all_to_all | solution.py:110
  37.5 4.2 reshape.274
  41.7 11.1 %all-to-all-start.1 = ((bf16[64,10,1536]{2,1,0:T(8,128)(2,1)}), bf16[64,10,1536]{2,1,0:T(8,128)(2,1)}, u32[]{:S(2)}, u32[]{:S(2)}) async-start(bf16[64,10,1536]{2,1,0:T(8,128)(2,1)} %reshape.274), calls=%async_computation.1 | async-start | bytes 6291456 | tf_op jit(solution)/shard_map/all_to_all | solution.py:108
  55.8 66.0 %all-to-all-done.1 = bf16[64,10,1536]{2,1,0:T(8,128)(2,1)} async-done(((bf16[64,10,1536]{2,1,0:T(8,128)(2,1)}), bf16[64,10,1536]{2,1,0:T(8,128)(2,1)}, u32[]{:S(2)}, u32[]{:S(2)}) %all-to-all-start.1) | async-done | bytes 1966112 | tf_op jit(solution)/shard_map/all_to_all | solution.py:108
  121.8 6.5 broadcast_in_dim.85
  128.3 10.5 %all-to-all-start.2 = ((bf16[64,2,24,1536]{3,2,1,0:T(8,128)(2,1)}), bf16[64,2,24,1536]{3,2,1,0:T(8,128)(2,1)}, u32[]{:S(2)}, u32[]{:S(2)}) async-start(bf16[64,2,24,1536]{3,2,1,0:T(8,128)(2,1)} %bitcast.77), calls=%async_computation.2 | async-start | bytes 18874368 | tf_op jit(solution)/shard_map/all_to_all | solution.py:100
  143.4 199.7 %all-to-all-done.2 = bf16[64,2,24,1536]{3,2,1,0:T(8,128)(2,1)} async-done(((bf16[64,2,24,1536]{3,2,1,0:T(8,128)(2,1)}), bf16[64,2,24,1536]{3,2,1,0:T(8,128)(2,1)}, u32[]{:S(2)}, u32[]{:S(2)}) %all-to-all-start.2) | async-done | bytes 9437216 | tf_op jit(solution)/shard_map/all_to_all | solution.py:100
  343.1 8.1 copy.44
  351.1 9.8 select_convert_fusion.1
  360.9 4.2 reshape.279
  365.1 11.4 %all-to-all-start.3 = ((bf16[64,10,1536]{2,1,0:T(8,128)(2,1)}), bf16[64,10,1536]{2,1,0:T(8,128)(2,1)}, u32[]{:S(2)}, u32[]{:S(2)}) async-start(bf16[64,10,1536]{2,1,0:T(8,128)(2,1)} %reshape.279), calls=%async_computation.3 | async-start | bytes 6291456 | tf_op jit(solution)/shard_map/all_to_all | solution.py:119
  378.9 5.0 mul.171
  384.2 61.5 %all-to-all-done.3 = bf16[64,10,1536]{2,1,0:T(8,128)(2,1)} async-done(((bf16[64,10,1536]{2,1,0:T(8,128)(2,1)}), bf16[64,10,1536]{2,1,0:T(8,128)(2,1)}, u32[]{:S(2)}, u32[]{:S(2)}) %all-to-all-start.3) | async-done | bytes 1966112 | tf_op jit(solution)/shard_map/all_to_all | solution.py:119
  445.7 4.3 reshape.280
  461.9 3.7 gather_fusion.5
  465.7 4.2 reshape.283
  469.9 11.0 %all-to-all-start.4 = ((bf16[64,10,1536]{2,1,0:T(8,128)(2,1)}), bf16[64,10,1536]{2,1,0:T(8,128)(2,1)}, u32[]{:S(2)}, u32[]{:S(2)}) async-start(bf16[64,10,1536]{2,1,0:T(8,128)(2,1)} %reshape.283), calls=%async_computation.4 | async-start | bytes 6291456 | tf_op jit(solution)/shard_map/all_to_all | solution.py:109
  480.8 4.2 reshape.380
  485.1 64.7 %all-to-all-done.4 = bf16[64,10,1536]{2,1,0:T(8,128)(2,1)} async-done(((bf16[64,10,1536]{2,1,0:T(8,128)(2,1)}), bf16[64,10,1536]{2,1,0:T(8,128)(2,1)}, u32[]{:S(2)}, u32[]{:S(2)}) %all-to-all-start.4) | async-done | bytes 1966112 | tf_op jit(solution)/shard_map/all_to_all | solution.py:109
  554.5 4.0 copy.46
  558.4 9.7 convolution_bitcast_fusion
  568.1 10.7 %all-to-all-start.6 = ((f32[1,64,24,1536]{3,2,0,1:T(8,128)}), f32[1,64,24,1536]{3,2,0,1:T(8,128)}, u32[]{:S(2)}, u32[]{:S(2)}) async-start(f32[1,64,24,1536]{3,2,0,1:T(8,128)} %convolution_bitcast_fusion), calls=%async_computation.6 | async-start | bytes 18874368 | tf_op jit(solution)/shard_map/all_to_all | solution.py:167
  580.2 205.3 %all-to-all-done.6 = f32[1,64,24,1536]{3,2,0,1:T(8,128)} async-done(((f32[1,64,24,1536]{3,2,0,1:T(8,128)}), f32[1,64,24,1536]{3,2,0,1:T(8,128)}, u32[]{:S(2)}, u32[]{:S(2)}) %all-to-all-start.6) | async-done | bytes 9437216 | tf_op jit(solution)/shard_map/all_to_all | solution.py:167
  785.5 5.2 reduce_sum.102
  793.8 6.3 broadcast_multiply_fusion
  801.6 9.6 select_convert_fusion
  811.3 4.2 reshape.285
  815.5 12.3 %all-to-all-start.5 = ((bf16[64,10,1536]{2,1,0:T(8,128)(2,1)}), bf16[64,10,1536]{2,1,0:T(8,128)(2,1)}, u32[]{:S(2)}, u32[]{:S(2)}) async-start(bf16[64,10,1536]{2,1,0:T(8,128)(2,1)} %reshape.285), calls=%async_computation.5 | async-start | bytes 6291456 | tf_op jit(solution)/shard_map/all_to_all | solution.py:126
  832.1 81.9 %all-reduce.7.cloned.1.call-done = f32[2880,32]{0,1:T(8,128)} async-done(((f32[2880,32]{0,1:T(8,128)}), f32[2880,32]{0,1:T(8,128)}) %all-reduce.7.cloned.1.call-update) | async-done | bytes 368656 | tf_op jit(solution)/shard_map/psum | solution.py:187
  915.8 4.2 reshape.286
  924.7 3.8 reshape.287
  928.5 75.4 %all-reduce.4 = (f32[32]{0:T(128)S(1)}, f32[32]{0:T(128)S(1)}) all-reduce(f32[32]{0:T(128)S(1)} %get-tuple-element.7, f32[32]{0:T(128)S(1)} %get-tuple-element.16), channel_id=1, replica_groups=mesh['ctx'=64,'rep'=4] {'ctx','rep'}, use_global_device_ids=true, to_apply=%region_14.15 | all-reduce | flops 64 | bytes 512 | tf_op jit(solution)/shard_map/psum | solution.py:187
  (109 shorter events, 62.2 us)
Async XLA Ops:
  8.0 375.8 %copy-start = (bf16[1,128,2880]{1,2,0:T(8,128)(2,1)S(1)}, bf16[1,128,2880]{1,2,0:T(8,128)(2,1)}, u32[]{:S(2)}) copy-start(bf16[1,128,2880]{1,2,0:T(8,128)(2,1)} %param.9) | copy-start | bytes 2211844
  10.8 20.2 %copy-start.7 = (bf16[1,128,4,1536]{3,2,1,0:T(4,128)(2,1)S(1)}, bf16[1,128,4,1536]{3,2,1,0:T(4,128)(2,1)}, u32[]{:S(2)}) copy-start(bf16[1,128,4,1536]{3,2,1,0:T(4,128)(2,1)} %param.12) | copy-start | bytes 4718596
  17.5 24.2 %all-to-all-start = ((s32[64,1,10]{2,1,0:T(1,128)}), s32[64,1,10]{2,1,0:T(1,128)S(1)}, u32[]{:S(2)}, u32[]{:S(2)}) async-start(s32[64,1,10]{2,1,0:T(1,128)} %bitcast.5), calls=%async_computation | async-start | bytes 65536 | tf_op jit(solution)/shard_map/all_to_all | solution.py:110
  41.7 11.1 %copy-start.12 = (s32[32]{0:T(128)S(1)}, s32[32]{0:T(128)}, u32[]{:S(2)}) copy-start(s32[32]{0:T(128)} %param.14) | copy-start | bytes 388
  41.7 12.0 %copy-start.2 = (bf16[32,24,1536]{2,1,0:T(8,128)(2,1)S(1)}, bf16[32,24,1536]{2,1,0:T(8,128)(2,1)}, u32[]{:S(2)}) copy-start(bf16[32,24,1536]{2,1,0:T(8,128)(2,1)} %param.16) | copy-start | bytes 7077892
  41.7 80.1 %all-to-all-start.1 = ((bf16[64,10,1536]{2,1,0:T(8,128)(2,1)}), bf16[64,10,1536]{2,1,0:T(8,128)(2,1)}, u32[]{:S(2)}, u32[]{:S(2)}) async-start(bf16[64,10,1536]{2,1,0:T(8,128)(2,1)} %reshape.274), calls=%async_computation.1 | async-start | bytes 6291456 | tf_op jit(solution)/shard_map/all_to_all | solution.py:108
  128.3 10.5 %copy-start.1 = (f32[32]{0:T(128)S(1)}, f32[32]{0:T(128)}, u32[]{:S(2)}) copy-start(f32[32]{0:T(128)} %param.15) | copy-start | bytes 388
  128.3 214.8 %all-to-all-start.2 = ((bf16[64,2,24,1536]{3,2,1,0:T(8,128)(2,1)}), bf16[64,2,24,1536]{3,2,1,0:T(8,128)(2,1)}, u32[]{:S(2)}, u32[]{:S(2)}) async-start(bf16[64,2,24,1536]{3,2,1,0:T(8,128)(2,1)} %bitcast.77), calls=%async_computation.2 | async-start | bytes 18874368 | tf_op jit(solution)/shard_map/all_to_all | solution.py:100
  365.1 11.4 %copy-start.9 = (bf16[1,128,1536]{2,1,0:T(8,128)(2,1)S(1)}, bf16[1,128,1536]{2,1,0:T(8,128)(2,1)}, u32[]{:S(2)}) copy-start(bf16[1,128,1536]{2,1,0:T(8,128)(2,1)} %param.17) | copy-start | bytes 1179652
  365.1 80.5 %all-to-all-start.3 = ((bf16[64,10,1536]{2,1,0:T(8,128)(2,1)}), bf16[64,10,1536]{2,1,0:T(8,128)(2,1)}, u32[]{:S(2)}, u32[]{:S(2)}) async-start(bf16[64,10,1536]{2,1,0:T(8,128)(2,1)} %reshape.279), calls=%async_computation.3 | async-start | bytes 6291456 | tf_op jit(solution)/shard_map/all_to_all | solution.py:119
  378.9 5.0 copy-start.8
  378.9 5.0 copy-start.13
  378.9 5.2 copy-start.11
  454.6 3.0 copy-start.10
  457.5 1.8 copy-start.5
  469.9 80.0 %all-to-all-start.4 = ((bf16[64,10,1536]{2,1,0:T(8,128)(2,1)}), bf16[64,10,1536]{2,1,0:T(8,128)(2,1)}, u32[]{:S(2)}, u32[]{:S(2)}) async-start(bf16[64,10,1536]{2,1,0:T(8,128)(2,1)} %reshape.283), calls=%async_computation.4 | async-start | bytes 6291456 | tf_op jit(solution)/shard_map/all_to_all | solution.py:109
  552.7 5.7 copy-start.3
  568.1 217.4 %all-to-all-start.6 = ((f32[1,64,24,1536]{3,2,0,1:T(8,128)}), f32[1,64,24,1536]{3,2,0,1:T(8,128)}, u32[]{:S(2)}, u32[]{:S(2)}) async-start(f32[1,64,24,1536]{3,2,0,1:T(8,128)} %convolution_bitcast_fusion), calls=%async_computation.6 | async-start | bytes 18874368 | tf_op jit(solution)/shard_map/all_to_all | solution.py:167
  578.9 335.2 %all-reduce.7.cloned.1.call-start = ((), (), s32[]{:S(2)}) async-start(), calls=%async_computation.8 | async-start | bytes 753664 | tf_op jit(solution)/shard_map/psum | solution.py:187
  580.2 424.2 %reduce-scatter.2.cloned.1.call-start = ((), (), s32[]{:S(2)}) async-start(), calls=%async_computation.9 | async-start | bytes 5898240 | tf_op jit(solution)/shard_map/reduce_scatter | solution.py:183
  800.1 1.5 copy-start.4
  815.5 13.6 %copy-start.6 = (bf16[128,4,1536]{2,1,0:T(4,128)(2,1)S(1)}, bf16[128,4,1536]{2,1,0:T(4,128)(2,1)}, u32[]{:S(2)}) copy-start(bf16[128,4,1536]{2,1,0:T(4,128)(2,1)} %copy-done.5) | copy-start | bytes 4718596
  815.5 100.3 %all-to-all-start.5 = ((bf16[64,10,1536]{2,1,0:T(8,128)(2,1)}), bf16[64,10,1536]{2,1,0:T(8,128)(2,1)}, u32[]{:S(2)}, u32[]{:S(2)}) async-start(bf16[64,10,1536]{2,1,0:T(8,128)(2,1)} %reshape.285), calls=%async_computation.5 | async-start | bytes 6291456 | tf_op jit(solution)/shard_map/all_to_all | solution.py:126
Sparse Core Ops, SparseCore 0:
  585.8 328.2 all-reduce.6
Sparse Core Ops, SparseCore 1:
  800.2 83.5 reduce-scatter.1
where the time goes:
time: 1020 us; the launch traced here: 1010 us
  waiting for transfers between devices  679 us (67%)
  local copies, waits for them, and re-layouts  104 us (10%)
  starting transfers between devices  80.5 us (8%)
  blocking collectives  75.4 us (7%)
  matrix products  33.5 us (3%)
  other arithmetic  25.9 us (3%)
  between operations  16.1 us (2%)
    all_to_all x1, waiting for transfers between devices, on_device(): lax.all_to_all(lane_grads.reshape(per_lane, ctx_count, row_share, hidden_...  205 us
    all_to_all x1, waiting for transfers between devices, on_device(): lax.all_to_all(outgoing, 'ctx', split_axis=0, concat_axis=2, tiled=True)  200 us
    psum x1, waiting for transfers between devices, on_device(): lax.psum((part_router_w, part_router_b, coef_part), ('ctx', 'rep'))  81.9 us
    psum x1, blocking collectives, on_device(): lax.psum((part_router_w, part_router_b, coef_part), ('ctx', 'rep'))  75.4 us
    all_to_all x1, waiting for transfers between devices, on_device(): lax.all_to_all(send_hidden, 'ctx', split_axis=0, concat_axis=0, tiled=True)  66 us
    all_to_all x1, waiting for transfers between devices, on_device(): lax.all_to_all(send_grad, 'ctx', split_axis=0, concat_axis=0, tiled=True)  64.7 us
    all_to_all x1, waiting for transfers between devices, on_device(): lax.all_to_all(out_rows.astype(jnp.bfloat16).reshape(ctx_count, capacity,...  61.5 us
  transfers between devices with their start and end apart: 9, of which 6 were waited for; matrix products, arithmetic and copies ran while one was open for 8% of the time, Pallas kernels for 0%

commit v1 on v0

--- a/solution.py
+++ b/solution.py
@@ -1,3 +1,4 @@
+import functools
 import math
 import jax
 import jax.numpy as jnp
@@ -5,6 +6,15 @@
 from jax.sharding import PartitionSpec as P
 
 MERGED = 16
+
+
+def figure_drive(xs, link_axis, axis_name):
+    for t in (link_axis, axis_name):
+        xs = jax.lax.psum(xs, axis_name=t)
+    return xs
+
+
+switch_the_quarters = functools.partial(figure_drive, link_axis="ctx", axis_name="rep")
 
 
 def expert_rows(rows_hidden, rows_grad, rows_member, lane_weights):
@@ -184,9 +194,7 @@
         source_grad * merge_coef[:, None, None], "rep", scatter_dimension=2, tiled=True
     )
     source_w_grad = summed * grad_scale
-    router_sum, bias_sum, coef_sum = lax.psum(
-        (part_router_w, part_router_b, coef_part), ("ctx", "rep")
-    )
+    router_sum, bias_sum, coef_sum = switch_the_quarters((part_router_w, part_router_b, coef_part))
     return (
         mixed,
         hidden_grad,

time: 1020 us -> 1440 us (1.41)
  waiting for transfers between devices: 679 us -> 996 us
  blocking collectives: 75.4 us -> 189 us
    psum x1 -> x2, waiting for transfers between devices: 81.9 us -> 604 us  [figure_drive(): xs = jax.lax.psum(xs, axis_name=t)]
    all_to_all x1, waiting for transfers between devices: 205 us -> 0.01 us  [on_device(): lax.all_to_all(lane_grads.reshape(per_lane, ctx_count, row_share, hidden_...]
    psum x1 -> x2, blocking collectives: 75.4 us -> 189 us  [figure_drive(): xs = jax.lax.psum(xs, axis_name=t)]
  transfers between devices with their start and end apart: 9 -> 10, of which waited for: 6 -> 6; matrix products, arithmetic and copies ran while one was open for 8% -> 6% of each run, Pallas kernels for 0% -> 0%
where the time goes in v1:
time: 1440 us
  waiting for transfers between devices  996 us (69%)
  blocking collectives  189 us (13%)
  local copies, waits for them, and re-layouts  104 us (7%)
  starting transfers between devices  74.2 us (5%)
  matrix products  33.5 us (2%)
  other arithmetic  25.9 us (2%)
  between operations  14.4 us (1%)
    psum x2, waiting for transfers between devices, figure_drive(): xs = jax.lax.psum(xs, axis_name=t)  604 us
    all_to_all x1, waiting for transfers between devices, on_device(): lax.all_to_all(outgoing, 'ctx', split_axis=0, concat_axis=2, tiled=True)  200 us
    psum x2, blocking collectives, figure_drive(): xs = jax.lax.psum(xs, axis_name=t)  189 us
    all_to_all x1, waiting for transfers between devices, on_device(): lax.all_to_all(send_hidden, 'ctx', split_axis=0, concat_axis=0, tiled=True)  66 us
    all_to_all x1, waiting for transfers between devices, on_device(): lax.all_to_all(send_grad, 'ctx', split_axis=0, concat_axis=0, tiled=True)  64.7 us
    all_to_all x1, waiting for transfers between devices, on_device(): lax.all_to_all(out_rows.astype(jnp.bfloat16).reshape(ctx_count, capacity,...  61.5 us
  transfers between devices with their start and end apart: 10, of which 6 were waited for; matrix products, arithmetic and copies ran while one was open for 6% of the time, Pallas kernels for 0%

profile of v1, /device:TPU:1, one launch (start us, length us, event | category | flops | bytes accessed | tf_op | source)
XLA Modules:
  0.0 1436.5 jit_solution(364385043876456273)
XLA Ops:
  16.6 13.5 all-to-all-start
  36.7 4.2 reshape.274
  40.9 11.1 all-to-all-start.1
  55.0 66.0 %all-to-all-done.1 = bf16[64,10,1536]{2,1,0:T(8,128)(2,1)} async-done(((bf16[64,10,1536]{2,1,0:T(8,128)(2,1)}), bf16[64,10,1536]{2,1,0:T(8,128)(2,1)}, u32[]{:S(2)}, u32[]{:S(2)}) %all-to-all-start.1) | async-done | bytes 1966112 | tf_op jit(solution)/shard_map/all_to_all | solution.py:118
  121.0 6.5 broadcast_in_dim.85
  127.5 10.5 all-to-all-start.2
  142.6 199.7 %all-to-all-done.2 = bf16[64,2,24,1536]{3,2,1,0:T(8,128)(2,1)} async-done(((bf16[64,2,24,1536]{3,2,1,0:T(8,128)(2,1)}), bf16[64,2,24,1536]{3,2,1,0:T(8,128)(2,1)}, u32[]{:S(2)}, u32[]{:S(2)}) %all-to-all-start.2) | async-done | bytes 9437216 | tf_op jit(solution)/shard_map/all_to_all | solution.py:110
  342.2 8.1 copy.44
  350.3 9.8 select_convert_fusion.1
  360.1 4.2 reshape.279
  364.3 11.4 all-to-all-start.3
  378.0 5.0 mul.171
  383.3 61.5 %all-to-all-done.3 = bf16[64,10,1536]{2,1,0:T(8,128)(2,1)} async-done(((bf16[64,10,1536]{2,1,0:T(8,128)(2,1)}), bf16[64,10,1536]{2,1,0:T(8,128)(2,1)}, u32[]{:S(2)}, u32[]{:S(2)}) %all-to-all-start.3) | async-done | bytes 1966112 | tf_op jit(solution)/shard_map/all_to_all | solution.py:129
  444.8 4.3 reshape.280
  464.8 4.2 reshape.283
  469.0 11.0 all-to-all-start.4
  480.0 4.2 reshape.380
  484.2 64.7 %all-to-all-done.4 = bf16[64,10,1536]{2,1,0:T(8,128)(2,1)} async-done(((bf16[64,10,1536]{2,1,0:T(8,128)(2,1)}), bf16[64,10,1536]{2,1,0:T(8,128)(2,1)}, u32[]{:S(2)}, u32[]{:S(2)}) %all-to-all-start.4) | async-done | bytes 1966112 | tf_op jit(solution)/shard_map/all_to_all | solution.py:119
  553.6 4.0 copy.46
  557.6 9.7 convolution_bitcast_fusion
  567.3 10.7 all-to-all-start.6
  579.4 559.0 %all-reduce.9.cloned.1.call-done = f32[2880,32]{0,1:T(8,128)} async-done(((f32[2880,32]{0,1:T(8,128)}), f32[2880,32]{0,1:T(8,128)}) %all-reduce.9.cloned.1.call-update) | async-done | bytes 368656 | tf_op jit(solution)/shard_map/psum | solution.py:13
  1138.5 5.2 reduce_sum.102
  1146.7 6.3 broadcast_multiply_fusion
  1154.6 9.6 select_convert_fusion
  1164.2 4.2 reshape.285
  1168.4 5.9 all-to-all-start.5
  1178.7 44.6 %all-reduce.11.cloned.1.call-done = f32[2880,32]{0,1:T(8,128)} async-done(((f32[2880,32]{0,1:T(8,128)}), f32[2880,32]{0,1:T(8,128)}) %all-reduce.11.cloned.1.call-update) | async-done | bytes 368656 | tf_op jit(solution)/shard_map/psum | solution.py:13
  1225.1 4.2 reshape.286
  1233.9 3.8 reshape.287
  1237.8 133.3 %all-reduce.4 = (f32[32]{0:T(128)S(1)}, f32[32]{0:T(128)S(1)}) all-reduce(f32[32]{0:T(128)S(1)} %get-tuple-element.7, f32[32]{0:T(128)S(1)} %get-tuple-element.18), channel_id=1, replica_groups=mesh['ctx'=64,'rep'=4] {'ctx'}, use_global_device_ids=true, to_apply=%region_15.16 | all-reduce | flops 64 | bytes 512 | tf_op jit(solution)/shard_map/psum | solution.py:13
  1371.1 55.7 %all-reduce.5 = (f32[32]{0:T(128)S(1)}, f32[32]{0:T(128)S(1)}) all-reduce(f32[32]{0:T(128)S(1)} %get-tuple-element.9, f32[32]{0:T(128)S(1)} %get-tuple-element.10), channel_id=1, replica_groups=mesh['ctx'=64,'rep'=4] {'rep'}, use_global_device_ids=true, to_apply=%region_16.17 | all-reduce | flops 64 | bytes 512 | tf_op jit(solution)/shard_map/psum | solution.py:13
  (113 shorter events, 66.0 us)
Async XLA Ops:
  7.2 375.8 %copy-start = (bf16[1,128,2880]{1,2,0:T(8,128)(2,1)S(1)}, bf16[1,128,2880]{1,2,0:T(8,128)(2,1)}, u32[]{:S(2)}) copy-start(bf16[1,128,2880]{1,2,0:T(8,128)(2,1)} %param.9) | copy-start | bytes 2211844
  10.0 20.2 %copy-start.7 = (bf16[1,128,4,1536]{3,2,1,0:T(4,128)(2,1)S(1)}, bf16[1,128,4,1536]{3,2,1,0:T(4,128)(2,1)}, u32[]{:S(2)}) copy-start(bf16[1,128,4,1536]{3,2,1,0:T(4,128)(2,1)} %param.12) | copy-start | bytes 4718596
  16.6 24.2 %all-to-all-start = ((s32[64,1,10]{2,1,0:T(1,128)}), s32[64,1,10]{2,1,0:T(1,128)S(1)}, u32[]{:S(2)}, u32[]{:S(2)}) async-start(s32[64,1,10]{2,1,0:T(1,128)} %bitcast.5), calls=%async_computation | async-start | bytes 65536 | tf_op jit(solution)/shard_map/all_to_all | solution.py:120
  40.9 11.1 copy-start.12
  40.9 12.0 copy-start.2
  40.9 80.1 %all-to-all-start.1 = ((bf16[64,10,1536]{2,1,0:T(8,128)(2,1)}), bf16[64,10,1536]{2,1,0:T(8,128)(2,1)}, u32[]{:S(2)}, u32[]{:S(2)}) async-start(bf16[64,10,1536]{2,1,0:T(8,128)(2,1)} %reshape.274), calls=%async_computation.1 | async-start | bytes 6291456 | tf_op jit(solution)/shard_map/all_to_all | solution.py:118
  127.5 10.5 copy-start.1
  127.5 214.8 %all-to-all-start.2 = ((bf16[64,2,24,1536]{3,2,1,0:T(8,128)(2,1)}), bf16[64,2,24,1536]{3,2,1,0:T(8,128)(2,1)}, u32[]{:S(2)}, u32[]{:S(2)}) async-start(bf16[64,2,24,1536]{3,2,1,0:T(8,128)(2,1)} %bitcast.77), calls=%async_computation.2 | async-start | bytes 18874368 | tf_op jit(solution)/shard_map/all_to_all | solution.py:110
  364.3 11.4 copy-start.9
  364.3 80.5 %all-to-all-start.3 = ((bf16[64,10,1536]{2,1,0:T(8,128)(2,1)}), bf16[64,10,1536]{2,1,0:T(8,128)(2,1)}, u32[]{:S(2)}, u32[]{:S(2)}) async-start(bf16[64,10,1536]{2,1,0:T(8,128)(2,1)} %reshape.279), calls=%async_computation.3 | async-start | bytes 6291456 | tf_op jit(solution)/shard_map/all_to_all | solution.py:129
  378.0 5.0 copy-start.8
  378.0 5.0 copy-start.13
  378.0 5.2 copy-start.11
  453.7 3.0 copy-start.10
  456.7 1.8 copy-start.5
  469.0 80.0 %all-to-all-start.4 = ((bf16[64,10,1536]{2,1,0:T(8,128)(2,1)}), bf16[64,10,1536]{2,1,0:T(8,128)(2,1)}, u32[]{:S(2)}, u32[]{:S(2)}) async-start(bf16[64,10,1536]{2,1,0:T(8,128)(2,1)} %reshape.283), calls=%async_computation.4 | async-start | bytes 6291456 | tf_op jit(solution)/shard_map/all_to_all | solution.py:119
  551.9 5.7 copy-start.3
  567.3 571.2 %all-to-all-start.6 = ((f32[1,64,24,1536]{3,2,0,1:T(8,128)}), f32[1,64,24,1536]{3,2,0,1:T(8,128)}, u32[]{:S(2)}, u32[]{:S(2)}) async-start(f32[1,64,24,1536]{3,2,0,1:T(8,128)} %convolution_bitcast_fusion), calls=%async_computation.6 | async-start | bytes 18874368 | tf_op jit(solution)/shard_map/all_to_all | solution.py:177
  578.0 560.4 %all-reduce.9.cloned.1.call-start = ((), (), s32[]{:S(2)}) async-start(), calls=%async_computation.8 | async-start | bytes 753664 | tf_op jit(solution)/shard_map/psum | solution.py:13
  579.3 644.0 %all-reduce.11.cloned.1.call-start = ((), (), s32[]{:S(2)}) async-start(), calls=%async_computation.9 | async-start | bytes 753664 | tf_op jit(solution)/shard_map/psum | solution.py:13
  1138.4 288.9 %reduce-scatter.2.cloned.1.call-start = ((), (), s32[]{:S(2)}) async-start(), calls=%async_computation.10 | async-start | bytes 5898240 | tf_op jit(solution)/shard_map/reduce_scatter | solution.py:193
  1153.0 1.5 copy-start.4
  1168.4 7.2 copy-start.6
  1168.4 56.7 %all-to-all-start.5 = ((bf16[64,10,1536]{2,1,0:T(8,128)(2,1)}), bf16[64,10,1536]{2,1,0:T(8,128)(2,1)}, u32[]{:S(2)}, u32[]{:S(2)}) async-start(bf16[64,10,1536]{2,1,0:T(8,128)(2,1)} %reshape.285), calls=%async_computation.5 | async-start | bytes 6291456 | tf_op jit(solution)/shard_map/all_to_all | solution.py:136
Sparse Core Ops, SparseCore 0:
  582.0 556.3 all-reduce.8
  1141.0 82.2 all-reduce.10
  1226.1 62.7 reduce-scatter.1
